TPU v7x, 32 devices: a whole 2x2x4 slice. The times are simulated.
32 devices in a mesh: kpt: 4 (over y, core), row: 4 (over z), col: 2 (over x).
Axes of the slice: x: 2, y: 2, z: 4, core: 2. Of those that a mesh axis runs over, the one named last changes fastest.
Arguments:
- a_matrix: bfloat16 [8, 4096, 4096], P('kpt', 'row', 'col'), parts along dimension 0, may hold values from -6 to 6
- b_matrix: bfloat16 [8, 4096, 4096], P('kpt', 'row', 'col'), parts along dimension 0, may hold values from -0.09375 to 0.09375
- a_level: int32 [128, 32], P('kpt'), parts along dimension 0, may hold values from 0 to 4, as said below
- b_level: int32 [128, 32], P('kpt'), parts along dimension 0, may hold values from 0 to 4, as said below
- limit: int32 [128, 32], P(('kpt', 'row'), 'col'), parts along dimension 0, may hold values from 3 to 8
Outputs:
- product: bfloat16 [8, 4096, 4096], P('kpt', 'row', 'col'), parts along dimension 0
- kept_count: int32 [128, 32], P(('kpt', 'row'), 'col'), parts along dimension 0
- kept_total: int32 [4], P('kpt'), parts along dimension 0
There are 4 independent parts, one for each index of `kpt`. A program takes and returns all parts, laid end to end along the dimension named above; each array names one. Nothing has to cross between parts.
Inputs may be any that keep to these rules, and one draw needn't show every extreme that they name: Each block's level is 0 (empty) or its norm exponent 1 to 4; the share of occupied blocks rises from some a sixth in the first block row of a_level (block column of b_level) to some six in seven in the last. `b_level`: as for a_level, with the share rising along block columns.
All inputs are finite; a program needn't handle non-finite values.
Results may differ from a plain program's by a relative error of at most 0.001.
Values may be sent and summed in bfloat16 or wider, within the bound.
No kernel may reach another device: no remote copies, remote signals or barrier semaphores. Data moves between devices by JAX's collectives and lax.ppermute only.
A program may use at most 576 MiB of HBM per device.

v0:
```python
import jax
import jax.numpy as jnp
from jax import lax
from jax.sharding import PartitionSpec as P

BLK = 128


def level_scale(levels):
    power = jnp.power(jnp.float32(2.0), (1 - levels).astype(jnp.float32))
    return jnp.where(levels > 0, power, jnp.float32(0.0))


def spread_blocks(small):
    return jnp.repeat(jnp.repeat(small, BLK, axis=0), BLK, axis=1)


def block_terms(a_piece, a_lev, b_piece, b_lev, limit):
    keep = (
        (a_lev[:, :, None] > 0)
        & (b_lev[None, :, :] > 0)
        & (a_lev[:, :, None] + b_lev[None, :, :] <= limit[:, None, :])
    )
    counted = jnp.sum(keep.astype(jnp.int32), axis=1)
    results = []
    for column in range(limit.shape[1]):
        mask = jnp.repeat(keep[:, :, column], BLK, axis=0)
        masked = jnp.where(mask[None], a_piece, jnp.zeros((), jnp.bfloat16))
        right = b_piece[:, :, column * BLK : (column + 1) * BLK]
        real_real = jnp.dot(masked[0], right[0], preferred_element_type=jnp.float32)
        imag_imag = jnp.dot(masked[1], right[1], preferred_element_type=jnp.float32)
        real_imag = jnp.dot(masked[0], right[1], preferred_element_type=jnp.float32)
        imag_real = jnp.dot(masked[1], right[0], preferred_element_type=jnp.float32)
        results.append(jnp.stack([real_real - imag_imag, real_imag + imag_real]))
    return (jnp.concatenate(results, axis=2), counted)


def shards(a_matrix, b_matrix, a_level, b_level, limit):
    row_place = lax.axis_index("row")
    col_place = lax.axis_index("col")
    row_blocks = a_matrix.shape[1] // BLK
    col_blocks = a_matrix.shape[2] // BLK
    a_own = lax.dynamic_slice(
        a_level, (row_place * row_blocks, col_place * col_blocks), (row_blocks, col_blocks)
    )
    b_own = lax.dynamic_slice(
        b_level, (row_place * row_blocks, col_place * col_blocks), (row_blocks, col_blocks)
    )
    a_eff = a_matrix * spread_blocks(level_scale(a_own)).astype(jnp.bfloat16)[None]
    b_eff = b_matrix * spread_blocks(level_scale(b_own)).astype(jnp.bfloat16)[None]
    a_band = lax.dynamic_slice_in_dim(a_level, row_place * row_blocks, row_blocks, 0)
    b_band = lax.dynamic_slice_in_dim(b_level, col_place * col_blocks, col_blocks, 1)
    a_levels = jnp.repeat(a_band, BLK, axis=1)
    b_levels = jnp.repeat(b_band, BLK, axis=0)
    a_whole = lax.all_gather(a_eff, "col", axis=2, tiled=True)
    added, counted = block_terms(
        a_whole, a_levels, lax.all_gather(b_eff, "row", axis=1, tiled=True), b_levels, limit
    )
    kept_count = counted // BLK
    kept_total = lax.psum(jnp.sum(kept_count).reshape(1), ("row", "col"))
    return (added.astype(jnp.bfloat16), kept_count, kept_total)


def solution(mesh):
    in_specs = (
        P("kpt", "row", "col"),
        P("kpt", "row", "col"),
        P("kpt", None),
        P("kpt", None),
        P(("kpt", "row"), "col"),
    )
    out_specs = (P("kpt", "row", "col"), P(("kpt", "row"), "col"), P("kpt"))
    return jax.shard_map(shards, mesh=mesh, in_specs=in_specs, out_specs=out_specs, check_vma=False)
```

profile of v0, /device:TPU:0, one launch (start us, length us, event | category | flops | bytes accessed | tf_op | source)
XLA Modules:
  0.0 1229.6 jit_solution(12622931891409190300)
XLA Ops:
  25.3 8.4 broadcast_multiply_fusion
  37.7 14.6 %psum.7 = s32[1]{0:T(128)} all-reduce(s32[1]{0:T(128)} %bitcast.131), channel_id=1, replica_groups=mesh['kpt'=4,'row'=4,'col'=2] {'row','col'}, use_global_device_ids=true, to_apply=%region_2.3 | all-reduce | flops 1 | bytes 8 | tf_op jit(solution)/shard_map/psum | solution.py:60
  52.3 168.1 %all-gather.3.cloned.1.call-done = bf16[2,1024,4096]{2,1,0:T(8,128)(2,1)} async-done(((bf16[2,1024,2048]{2,1,0:T(8,128)(2,1)}), bf16[2,1024,4096]{2,1,0:T(8,128)(2,1)}) %all-gather.3.cloned.1.call-update) | async-done | bytes 16777232 | tf_op jit(solution)/shard_map/all_gather | solution.py:55
  285.2 115.4 %broadcast_select_fusion = (bf16[2,1024,4096]{2,1,0:T(8,128)(2,1)}, bf16[2,1024,4096]{2,1,0:T(8,128)(2,1)}, bf16[2,1024,4096]{2,1,0:T(8,128)(2,1)}, bf16[2,1024,...) fusion(bf16[2,1024,4096]{2,1,0:T(8,128)(2,1)} %all-gather.3.clo, ...), kind=kLoop, calls=%fused_computation | loop fusion | flops 134217728 | bytes 352321536 | tf_op jit(solution)/shard_map/jit(_where)/select_n | solution.py:28
  400.6 382.8 %all-gather.5.cloned.1.call-done = bf16[2,4096,2048]{2,1,0:T(8,128)(2,1)} async-done(((bf16[2,1024,2048]{2,1,0:T(8,128)(2,1)}), bf16[2,4096,2048]{2,1,0:T(8,128)(2,1)}) %all-gather.5.cloned.1.call-update) | async-done | bytes 33554448 | tf_op jit(solution)/shard_map/all_gather | solution.py:57
  783.4 6.7 fusion.1
  818.1 6.7 fusion.157
  859.0 6.7 fusion.13
  865.8 6.5 fusion.12
  892.6 6.5 fusion.16
  899.2 6.9 fusion.151
  919.9 6.5 fusion.20
  940.3 6.7 fusion.25
  973.9 6.5 fusion.28
  980.4 6.7 fusion.145
  1021.3 6.9 fusion.37
  1055.1 6.5 fusion.40
  1061.7 6.7 fusion.139
  1082.2 6.5 fusion.44
  1102.6 6.7 fusion.49
  1136.2 6.5 fusion.52
  1142.7 6.9 fusion.133
  1190.3 6.7 fusion.60
  1210.9 11.6 copy.28
  (112 shorter events, 394.1 us)
Async XLA Ops:
  7.2 213.3 %all-gather.3.cloned.1.call-start = ((), (), s32[]{:S(2)}) async-start(), calls=%async_computation | async-start | bytes 25165824 | tf_op jit(solution)/shard_map/all_gather | solution.py:55
  7.2 7.6 copy-start.1
  18.6 764.8 %all-gather.5.cloned.1.call-start = ((), (), s32[]{:S(2)}) async-start(), calls=%async_computation.1 | async-start | bytes 41943040 | tf_op jit(solution)/shard_map/all_gather | solution.py:57
  25.3 8.4 copy-start.2
  25.3 9.6 copy-start.3
  783.4 8.5 copy-start
Sparse Core Ops, SparseCore 0:
  18.7 201.6 all-gather.2
  222.0 561.3 all-gather.4
where the time goes:
time: 1240 us; the launch traced here: 1230 us
  waiting for transfers between devices  551 us (44%)
  matrix products  412 us (33%)
  other arithmetic  144 us (12%)
  local copies, waits for them, and re-layouts  92.9 us (7%)
  between operations  14.8 us (1%)
  blocking collectives  14.6 us (1%)
    all_gather x1, waiting for transfers between devices, shards(): lax.all_gather(b_eff, 'row', axis=1, tiled=True)  383 us
    all_gather x1, waiting for transfers between devices, shards(): a_whole = lax.all_gather(a_eff, 'col', axis=2, tiled=True)  168 us
    select_n x1, other arithmetic, block_terms(): masked = jnp.where(mask[None], a_piece, jnp.zeros((), jnp.bfloat16))  115 us
    dot_general x16, matrix products, block_terms(): real_real = jnp.dot(masked[0], right[0], preferred_element_type=jnp.float32)  105 us
    dot_general x16, matrix products, block_terms(): imag_imag = jnp.dot(masked[1], right[1], preferred_element_type=jnp.float32)  103 us
    dot_general x16, matrix products, block_terms(): real_imag = jnp.dot(masked[0], right[1], preferred_element_type=jnp.float32)  102 us
    dot_general x16, matrix products, block_terms(): imag_real = jnp.dot(masked[1], right[0], preferred_element_type=jnp.float32)  102 us
    broadcast_in_dim x16, local copies, waits for them, and re-layouts, block_terms(): mask = jnp.repeat(keep[:, :, column], BLK, axis=0)  64.8 us
  transfers between devices with their start and end apart: 2, of which 2 were waited for; matrix products, arithmetic and copies ran while one was open for 16% of the time, Pallas kernels for 0%

commit v1 on v0

--- a/solution.py
+++ b/solution.py
@@ -52,7 +52,7 @@
     b_band = lax.dynamic_slice_in_dim(b_level, col_place * col_blocks, col_blocks, 1)
     a_levels = jnp.repeat(a_band, BLK, axis=1)
     b_levels = jnp.repeat(b_band, BLK, axis=0)
-    a_whole = lax.all_gather(a_eff, "col", axis=2, tiled=True)
+    a_whole = jnp.concatenate(lax.all_gather(a_eff, "col"), axis=2)
     added, counted = block_terms(
         a_whole, a_levels, lax.all_gather(b_eff, "row", axis=1, tiled=True), b_levels, limit
     )

time: 1240 us -> 1010 us (0.81)
  matrix products: 412 us -> 177 us
  local copies, waits for them, and re-layouts: 92.9 us -> 325 us
  waiting for transfers between devices: 551 us -> 324 us
    all_gather x1, waiting for transfers between devices: 168 us -> 0.01 us  [shards(): a_whole = jnp.concatenate(lax.all_gather(a_eff, 'col'), axis=2)]
    broadcast_in_dim x16, local copies, waits for them, and re-layouts: 64.8 us -> 194 us  [block_terms(): mask = jnp.repeat(keep[:, :, column], BLK, axis=0)]
    dot_general x16, matrix products: 105 us -> 44.8 us  [block_terms(): real_real = jnp.dot(masked[0], right[0], preferred_element_type=jnp.float32)]
    dot_general x16, matrix products: 102 us -> 42.8 us  [block_terms(): real_imag = jnp.dot(masked[0], right[1], preferred_element_type=jnp.float32)]
    all_gather x1, waiting for transfers between devices: 383 us -> 324 us  [shards(): lax.all_gather(b_eff, 'row', axis=1, tiled=True)]
    dot_general x16, matrix products: 103 us -> 45 us  [block_terms(): imag_imag = jnp.dot(masked[1], right[1], preferred_element_type=jnp.float32)]
    dot_general x16, matrix products: 102 us -> 44.6 us  [block_terms(): imag_real = jnp.dot(masked[1], right[0], preferred_element_type=jnp.float32)]
    broadcast_in_dim x0 -> x8, local copies, waits for them, and re-layouts: none -> 55.2 us  [block_terms(): masked = jnp.where(mask[None], a_piece, jnp.zeros((), jnp.bfloat16))]
  transfers between devices with their start and end apart: 2 -> 2, of which waited for: 2 -> 1; matrix products, arithmetic and copies ran while one was open for 16% -> 42% of each run, Pallas kernels for 0% -> 0%
where the time goes in v1:
time: 1010 us; the launch traced here: 1000 us
  local copies, waits for them, and re-layouts  325 us (32%)
  waiting for transfers between devices  324 us (32%)
  matrix products  177 us (18%)
  other arithmetic  144 us (14%)
  between operations  15.6 us (2%)
  blocking collectives  15 us (1%)
    all_gather x1, waiting for transfers between devices, shards(): lax.all_gather(b_eff, 'row', axis=1, tiled=True)  324 us
    broadcast_in_dim x16, local copies, waits for them, and re-layouts, block_terms(): mask = jnp.repeat(keep[:, :, column], BLK, axis=0)  194 us
    select_n x1, other arithmetic, block_terms(): masked = jnp.where(mask[None], a_piece, jnp.zeros((), jnp.bfloat16))  115 us
    broadcast_in_dim x8, local copies, waits for them, and re-layouts, block_terms(): masked = jnp.where(mask[None], a_piece, jnp.zeros((), jnp.bfloat16))  55.2 us
    dot_general x16, matrix products, block_terms(): imag_imag = jnp.dot(masked[1], right[1], preferred_element_type=jnp.float32)  45 us
    dot_general x16, matrix products, block_terms(): real_real = jnp.dot(masked[0], right[0], preferred_element_type=jnp.float32)  44.8 us
    dot_general x16, matrix products, block_terms(): imag_real = jnp.dot(masked[1], right[0], preferred_element_type=jnp.float32)  44.6 us
    dot_general x16, matrix products, block_terms(): real_imag = jnp.dot(masked[0], right[1], preferred_element_type=jnp.float32)  42.8 us
  transfers between devices with their start and end apart: 2, of which 1 were waited for; matrix products, arithmetic and copies ran while one was open for 42% of the time, Pallas kernels for 0%

profile of v1, /device:TPU:0, one launch (start us, length us, event | category | flops | bytes accessed | tf_op | source)
XLA Modules:
  0.0 1001.5 jit_solution(7514053532873286338)
XLA Ops:
  25.3 8.4 broadcast_multiply_fusion
  38.3 15.0 %psum.7 = s32[1]{0:T(128)} all-reduce(s32[1]{0:T(128)} %bitcast.118), channel_id=1, replica_groups=mesh['kpt'=4,'row'=4,'col'=2] {'row','col'}, use_global_device_ids=true, to_apply=%region_2.3 | all-reduce | flops 1 | bytes 8 | tf_op jit(solution)/shard_map/psum | solution.py:60
  72.5 11.4 %broadcast_in_dim.258 = pred[8,128,4096]{1,0,2:T(8,128)(4,1)S(1)} broadcast(pred[8,4096]{0,1:T(8,128)(4,1)} %copy.94), dimensions={0,2} | broadcast | bytes 4227072 | tf_op jit(solution)/shard_map/broadcast_in_dim | solution.py:27
  84.0 11.2 %broadcast_in_dim.261 = pred[8,128,4096]{1,0,2:T(8,128)(4,1)S(1)} broadcast(pred[8,4096]{0,1:T(8,128)(4,1)} %copy.95), dimensions={0,2} | broadcast | bytes 4227072 | tf_op jit(solution)/shard_map/broadcast_in_dim | solution.py:27
  95.2 6.9 copy_bitcast_fusion
  102.2 12.1 %broadcast_in_dim.252 = pred[8,128,4096]{1,0,2:T(8,128)(4,1)S(1)} broadcast(pred[8,4096]{0,1:T(8,128)(4,1)S(1)} %copy-done.8), dimensions={0,2} | broadcast | bytes 4227072 | tf_op jit(solution)/shard_map/broadcast_in_dim | solution.py:27
  114.3 12.2 %broadcast_in_dim.255 = pred[8,128,4096]{1,0,2:T(8,128)(4,1)S(1)} broadcast(pred[8,4096]{0,1:T(8,128)(4,1)S(1)} %copy-done.9), dimensions={0,2} | broadcast | bytes 4227072 | tf_op jit(solution)/shard_map/broadcast_in_dim | solution.py:27
  133.5 12.1 %broadcast_in_dim.246 = pred[8,128,4096]{1,0,2:T(8,128)(4,1)S(1)} broadcast(pred[8,4096]{0,1:T(8,128)(4,1)S(1)} %copy-done.6), dimensions={0,2} | broadcast | bytes 4227072 | tf_op jit(solution)/shard_map/broadcast_in_dim | solution.py:27
  145.7 12.2 %broadcast_in_dim.249 = pred[8,128,4096]{1,0,2:T(8,128)(4,1)S(1)} broadcast(pred[8,4096]{0,1:T(8,128)(4,1)S(1)} %copy-done.7), dimensions={0,2} | broadcast | bytes 4227072 | tf_op jit(solution)/shard_map/broadcast_in_dim | solution.py:27
  164.8 12.1 %broadcast_in_dim.240 = pred[8,128,4096]{1,0,2:T(8,128)(4,1)S(1)} broadcast(pred[8,4096]{0,1:T(8,128)(4,1)S(1)} %copy-done.4), dimensions={0,2} | broadcast | bytes 4227072 | tf_op jit(solution)/shard_map/broadcast_in_dim | solution.py:27
  177.0 12.2 %broadcast_in_dim.243 = pred[8,128,4096]{1,0,2:T(8,128)(4,1)S(1)} broadcast(pred[8,4096]{0,1:T(8,128)(4,1)S(1)} %copy-done.5), dimensions={0,2} | broadcast | bytes 4227072 | tf_op jit(solution)/shard_map/broadcast_in_dim | solution.py:27
  189.2 6.9 copy_bitcast_fusion.6
  196.1 12.6 %broadcast_in_dim.234 = pred[8,128,4096]{1,0,2:T(8,128)(4,1)S(1)} broadcast(pred[8,4096]{0,1:T(8,128)(4,1)S(1)} %copy-done.2), dimensions={0,2} | broadcast | bytes 4227072 | tf_op jit(solution)/shard_map/broadcast_in_dim | solution.py:27
  208.7 12.2 %broadcast_in_dim.237 = pred[8,128,4096]{1,0,2:T(8,128)(4,1)S(1)} broadcast(pred[8,4096]{0,1:T(8,128)(4,1)S(1)} %copy-done.3), dimensions={0,2} | broadcast | bytes 4227072 | tf_op jit(solution)/shard_map/broadcast_in_dim | solution.py:27
  227.9 12.1 %broadcast_in_dim.228 = pred[8,128,4096]{1,0,2:T(8,128)(4,1)S(1)} broadcast(pred[8,4096]{0,1:T(8,128)(4,1)S(1)} %copy.84), dimensions={0,2} | broadcast | bytes 4227072 | tf_op jit(solution)/shard_map/broadcast_in_dim | solution.py:27
  240.0 12.2 %broadcast_in_dim.231 = pred[8,128,4096]{1,0,2:T(8,128)(4,1)S(1)} broadcast(pred[8,4096]{0,1:T(8,128)(4,1)S(1)} %copy.85), dimensions={0,2} | broadcast | bytes 4227072 | tf_op jit(solution)/shard_map/broadcast_in_dim | solution.py:27
  259.1 12.1 %broadcast_in_dim.222 = pred[8,128,4096]{1,0,2:T(8,128)(4,1)S(1)} broadcast(pred[8,4096]{0,1:T(8,128)(4,1)S(1)} %copy.82), dimensions={0,2} | broadcast | bytes 4227072 | tf_op jit(solution)/shard_map/broadcast_in_dim | solution.py:27
  271.3 12.2 %broadcast_in_dim.225 = pred[8,128,4096]{1,0,2:T(8,128)(4,1)S(1)} broadcast(pred[8,4096]{0,1:T(8,128)(4,1)S(1)} %copy.83), dimensions={0,2} | broadcast | bytes 4227072 | tf_op jit(solution)/shard_map/broadcast_in_dim | solution.py:27
  290.4 12.1 %broadcast_in_dim.210 = pred[8,128,4096]{1,0,2:T(8,128)(4,1)S(1)} broadcast(pred[8,4096]{0,1:T(8,128)(4,1)S(1)} %copy.79), dimensions={0,2} | broadcast | bytes 4227072 | tf_op jit(solution)/shard_map/broadcast_in_dim | solution.py:27
  302.5 12.2 %broadcast_in_dim.219 = pred[8,128,4096]{1,0,2:T(8,128)(4,1)S(1)} broadcast(pred[8,4096]{0,1:T(8,128)(4,1)S(1)} %copy.81), dimensions={0,2} | broadcast | bytes 4227072 | tf_op jit(solution)/shard_map/broadcast_in_dim | solution.py:27
  321.5 22.6 %copy.80 = bf16[2,1024,2,2048]{1,3,2,0:T(8,128)(2,1)} copy(bf16[2,1024,2,2048]{3,1,0,2:T(8,128)(2,1)} %bitcast.668) | data formatting | bytes 33554432 | tf_op jit(solution)/shard_map/reshape | solution.py:55
  344.1 115.4 %bitcast_select_fusion = (bf16[2,1024,4096]{1,2,0:T(8,128)(2,1)}, bf16[2,1024,4096]{1,2,0:T(8,128)(2,1)}, bf16[2,1024,4096]{1,2,0:T(8,128)(2,1)}, bf16[2,1024,40...) fusion(bf16[2,1024,2,2048]{1,3,2,0:T(8,128)(2,1)} %copy.80, ...), kind=kLoop, calls=%fused_computation | loop fusion | flops 134217728 | bytes 352321536 | tf_op jit(solution)/shard_map/jit(_where)/select_n | solution.py:28
  459.5 323.9 %all-gather.4.cloned.1.call-done = bf16[2,4096,2048]{2,1,0:T(8,128)(2,1)} async-done(((bf16[2,1024,2048]{2,1,0:T(8,128)(2,1)}), bf16[2,4096,2048]{2,1,0:T(8,128)(2,1)}) %all-gather.4.cloned.1.call-update) | async-done | bytes 33554448 | tf_op jit(solution)/shard_map/all_gather | solution.py:57
  982.8 11.6 %copy.100 = bf16[2,1024,2048]{2,1,0:T(8,128)(2,1)} copy(bf16[2,1024,2048]{1,2,0:T(8,128)(2,1)} %maximum_dynamic-update-slice_fusion) | data formatting | bytes 16777216
  (288 shorter events, 281.6 us)
Async XLA Ops:
  7.2 314.4 %all-gather.6.cloned.1.call-start = ((), (), s32[]{:S(2)}) async-start(), calls=%async_computation.1 | async-start | bytes 25165824 | tf_op jit(solution)/shard_map/all_gather | solution.py:55
  7.2 7.6 copy-start.1
  18.6 764.8 %all-gather.4.cloned.1.call-start = ((), (), s32[]{:S(2)}) async-start(), calls=%async_computation | async-start | bytes 41943040 | tf_op jit(solution)/shard_map/all_gather | solution.py:57
  95.2 7.0 copy-start.8
  95.2 19.1 %copy-start.9 = (pred[8,4096]{0,1:T(8,128)(4,1)S(1)}, pred[8,4096]{0,1:T(8,128)(4,1)}, u32[]{:S(2)}) copy-start(pred[8,4096]{0,1:T(8,128)(4,1)} %copy.93) | copy-start | bytes 98308
  126.6 6.9 copy-start.6
  126.6 19.1 %copy-start.7 = (pred[8,4096]{0,1:T(8,128)(4,1)S(1)}, pred[8,4096]{0,1:T(8,128)(4,1)}, u32[]{:S(2)}) copy-start(pred[8,4096]{0,1:T(8,128)(4,1)} %copy.91) | copy-start | bytes 98308
  157.9 6.9 copy-start.4
  157.9 19.1 %copy-start.5 = (pred[8,4096]{0,1:T(8,128)(4,1)S(1)}, pred[8,4096]{0,1:T(8,128)(4,1)}, u32[]{:S(2)}) copy-start(pred[8,4096]{0,1:T(8,128)(4,1)} %copy.89) | copy-start | bytes 98308
  189.2 6.9 copy-start.2
  189.2 19.5 %copy-start.3 = (pred[8,4096]{0,1:T(8,128)(4,1)S(1)}, pred[8,4096]{0,1:T(8,128)(4,1)}, u32[]{:S(2)}) copy-start(pred[8,4096]{0,1:T(8,128)(4,1)} %copy.87) | copy-start | bytes 98308
  783.4 8.5 copy-start
  843.0 6.9 slice-start.40
  843.0 6.9 slice-start.41
  867.4 6.6 slice-start.32
  867.4 6.6 slice-start.33
  891.5 6.5 slice-start.24
  915.8 6.5 slice-start.16
  915.8 6.5 slice-start.17
  928.3 6.5 slice-start.12
  928.4 6.5 slice-start.13
  940.4 6.5 slice-start.8
  952.4 6.7 slice-start.4
  952.5 6.7 slice-start.5
  (50 other events, 233.3 us)
Sparse Core Ops, SparseCore 0:
  18.7 201.6 all-gather.5
  222.0 561.3 all-gather.3
